TPU v7x, 256 devices: a whole 4x4x8 slice. The times are simulated.
256 devices in a mesh: shard: 32 (over z, x), tensor: 4 (over y), section: 2 (over core).
Axes of the slice: x: 4, y: 4, z: 8, core: 2. Of those that a mesh axis runs over, the one named last changes fastest.
Arguments:
- grad_parts: bfloat16 [8, 32, 1024, 1024], P(('tensor', 'section'), None, 'shard')
- weights: bfloat16 [32, 1024, 1024], P(None, 'shard', ('tensor', 'section')), may hold values from -6 to 6
- adam_m: float32 [32, 1024, 1024], P(None, 'shard', ('tensor', 'section'))
- adam_v: float32 [32, 1024, 1024], P(None, 'shard', ('tensor', 'section')), may hold values from 0.01 to 1
- left_stat: float32 [96, 1024, 1024], P('shard', None, ('tensor', 'section')), may hold values from -18 to 18
- right_stat: float32 [96, 1024, 1024], P('shard', None, ('tensor', 'section')), may hold values from -18 to 18
- left_root: bfloat16 [32, 1024, 1024], P(None, 'shard', ('tensor', 'section')), as said below
- right_root: bfloat16 [32, 1024, 1024], P(None, 'shard', ('tensor', 'section')), as said below
- block_owner: int32 [32], replicated, may hold values from 0 to 31, as said below
- block_matrix: int32 [32], replicated, may hold values from 0 to 4, as said below
- factors: float32 [832, 2048], P('shard', ('tensor', 'section')), may hold values from -6 to 6
- factor_grad: bfloat16 [832, 2048], P('shard', ('tensor', 'section')), may hold values from -6 to 6
- factor_m: float32 [832, 2048], P('shard', ('tensor', 'section')), may hold values from -3 to 3
- factor_v: float32 [832, 2048], P('shard', ('tensor', 'section')), may hold values from 0.2 to 2
Outputs:
- new_weights: bfloat16 [32, 1024, 1024], P(None, 'shard')
- adam_m_new: float32 [32, 1024, 1024], P(None, 'shard', ('tensor', 'section'))
- adam_v_new: float32 [32, 1024, 1024], P(None, 'shard', ('tensor', 'section'))
- left_new: float32 [96, 1024, 1024], P('shard', None, ('tensor', 'section'))
- right_new: float32 [96, 1024, 1024], P('shard', None, ('tensor', 'section'))
- factors_new: float32 [832, 2048], P('shard', ('tensor', 'section'))
- factor_m_new: float32 [832, 2048], P('shard', ('tensor', 'section'))
- factor_v_new: float32 [832, 2048], P('shard', ('tensor', 'section'))
Inputs may be any that keep to these rules, and one draw needn't show every extreme that they name: `block_owner`: no owner holds more than 3 blocks, and some owner holds exactly 3. `block_matrix`: matrices 0 to 3 hold 4 blocks each, all other blocks belong to matrix 4. `left_root`: every block is symmetric. `right_root`: every block is symmetric.
All inputs are finite; a program needn't handle non-finite values.
Results may differ from a plain program's by a relative error of at most 0.014.
Values may be sent and summed in bfloat16 or wider, within the bound.
A program may use at most 128 MiB of HBM per device.

v0:
```python
import jax
import jax.numpy as jnp
from jax import lax
from jax.sharding import PartitionSpec as P

B = 1024
MATS = 5
BETA_ONE = 0.9
BETA_TWO = 0.95
BETA_STAT = 0.95
LEARNING = 0.1
DECAY_RATE = 0.1
EPSILON = 1e-08
FLOOR_RATE = 1e-06
CORRECT_ONE = 1.0 - 0.9**10
CORRECT_TWO = 1.0 - 0.95**10


def adam_direction(grad_float, moment, second):
    moment_new = BETA_ONE * moment + (1.0 - BETA_ONE) * grad_float
    second_new = BETA_TWO * second + (1.0 - BETA_TWO) * grad_float * grad_float
    direction = moment_new / CORRECT_ONE / (jnp.sqrt(second_new / CORRECT_TWO) + EPSILON)
    return (moment_new, second_new, direction)


def slot_numbers(block_owner, capacity):
    positions = jnp.arange(block_owner.shape[0], dtype=jnp.int32)
    earlier = (block_owner[:, None] == block_owner[None, :]) & (
        positions[None, :] < positions[:, None]
    )
    return block_owner * capacity + jnp.sum(earlier.astype(jnp.int32), axis=1)


def slot_contents(slot, slot_total):
    positions = jnp.arange(slot.shape[0], dtype=jnp.int32)
    matches = jnp.arange(slot_total, dtype=jnp.int32)[:, None] == slot[None, :]
    occupied = jnp.any(matches, axis=1)
    block_ids = jnp.sum(jnp.where(matches, positions[None, :], 0), axis=1)
    return (block_ids, occupied)


def fill_slots(tiles, block_ids, occupied):
    picked = jnp.take(tiles, block_ids, axis=0)
    return jnp.where(occupied[:, None, None], picked, jnp.zeros_like(picked))


def shards(
    grad_parts,
    weights,
    adam_m,
    adam_v,
    left_stat,
    right_stat,
    left_root,
    right_root,
    block_owner,
    block_matrix,
    factors,
    factor_grad,
    factor_m,
    factor_v,
):
    capacity = left_stat.shape[0]
    owners = lax.axis_size("shard")
    owner_index = lax.axis_index("shard")
    group_index = lax.axis_index(("tensor", "section"))
    partials = grad_parts[0].astype(jnp.float32)
    gradient = lax.psum_scatter(
        partials.astype(jnp.bfloat16), ("tensor", "section"), scatter_dimension=2, tiled=True
    )
    gradient = lax.optimization_barrier(gradient)
    grad_float = gradient.astype(jnp.float32)
    adam_m_new, adam_v_new, direction = adam_direction(grad_float, adam_m, adam_v)
    matrix_range = jnp.arange(MATS, dtype=jnp.int32)
    onehot = (block_matrix[:, None] == matrix_range[None, :]).astype(jnp.float32)
    adam_part = jnp.sum(jnp.sum(direction * direction, axis=(1, 2))[:, None] * onehot, axis=0)
    slot = slot_numbers(block_owner, capacity)
    block_ids, occupied = slot_contents(slot, owners * capacity)
    slab_width = gradient.shape[2]

    def to_block(x):
        return lax.all_to_all(x, "shard", split_axis=0, concat_axis=1, tiled=True)

    left_cols = to_block(left_root)
    right_cols = to_block(right_root)
    left_full = lax.all_gather(left_cols, ("tensor", "section"), axis=2, tiled=True)
    grad_cols = to_block(gradient)
    mixed = jnp.einsum(
        "sij,sjc->sic", left_full, grad_cols, preferred_element_type=jnp.float32
    ).astype(jnp.bfloat16)
    mixed_full = lax.all_gather(mixed, ("tensor", "section"), axis=2, tiled=True)
    precond = jnp.einsum("sik,skc->sic", mixed_full, right_cols, preferred_element_type=jnp.float32)
    own_matrix = lax.dynamic_slice_in_dim(block_matrix, owner_index, 1)
    own_onehot = (own_matrix == matrix_range).astype(jnp.float32)
    shampoo_part = jnp.sum(precond * precond) * own_onehot
    precond_tile = lax.all_to_all(
        precond.astype(jnp.bfloat16), "shard", split_axis=1, concat_axis=0, tiled=True
    ).astype(jnp.float32)
    slot_cols = to_block(fill_slots(gradient, block_ids, occupied))
    grad_full = lax.all_gather(slot_cols, ("tensor", "section"), axis=2, tiled=True)
    first_row = group_index * slab_width
    grad_rows_own = lax.dynamic_slice_in_dim(grad_full, first_row, slab_width, 1)
    gram_left = jnp.einsum(
        "sik,sjk->sij", grad_full, grad_rows_own, preferred_element_type=jnp.float32
    )
    gram_right = jnp.einsum(
        "ski,skj->sij", grad_full, slot_cols, preferred_element_type=jnp.float32
    )
    left_new = BETA_STAT * left_stat + (1.0 - BETA_STAT) * gram_left
    right_new = BETA_STAT * right_stat + (1.0 - BETA_STAT) * gram_right
    adam_norm, shampoo_norm = lax.psum((adam_part, shampoo_part), ("shard", "tensor", "section"))
    counts = jnp.sum(onehot, axis=0) * float(B * B)
    graft_scale = jnp.sqrt(adam_norm / (shampoo_norm + FLOOR_RATE * counts))
    block_scale = jnp.sum(onehot * graft_scale[None, :], axis=1)
    weights_float = weights.astype(jnp.float32)
    updated = (
        weights_float
        - LEARNING * (block_scale[:, None, None] * precond_tile + DECAY_RATE * weights_float)
    ).astype(jnp.bfloat16)
    factor_m_new, factor_v_new, factor_step = adam_direction(
        factor_grad.astype(jnp.float32), factor_m, factor_v
    )
    factors_new = factors - LEARNING * (factor_step + DECAY_RATE * factors)
    new_weights = lax.all_gather(updated, ("tensor", "section"), axis=2, tiled=True)
    return (
        new_weights,
        adam_m_new,
        adam_v_new,
        left_new,
        right_new,
        factors_new,
        factor_m_new,
        factor_v_new,
    )


def solution(mesh):
    in_specs = (
        P(("tensor", "section"), None, "shard", None),
        P(None, "shard", ("tensor", "section")),
        P(None, "shard", ("tensor", "section")),
        P(None, "shard", ("tensor", "section")),
        P("shard", None, ("tensor", "section")),
        P("shard", None, ("tensor", "section")),
        P(None, "shard", ("tensor", "section")),
        P(None, "shard", ("tensor", "section")),
        P(),
        P(),
        P("shard", ("tensor", "section")),
        P("shard", ("tensor", "section")),
        P("shard", ("tensor", "section")),
        P("shard", ("tensor", "section")),
    )
    out_specs = (
        P(None, "shard", None),
        P(None, "shard", ("tensor", "section")),
        P(None, "shard", ("tensor", "section")),
        P("shard", None, ("tensor", "section")),
        P("shard", None, ("tensor", "section")),
        P("shard", ("tensor", "section")),
        P("shard", ("tensor", "section")),
        P("shard", ("tensor", "section")),
    )
    return jax.shard_map(shards, mesh=mesh, in_specs=in_specs, out_specs=out_specs, check_vma=False)
```

profile of v0, /device:TPU:1, one launch (start us, length us, event | category | flops | bytes accessed | tf_op | source)
XLA Modules:
  0.0 326.8 jit_solution(6027712454618299210)
XLA Ops:
  7.2 0.0 reduce-scatter.4.cloned.1.call-start
  7.2 12.5 %copy.31 = bf16[32,32,1024]{1,0,2:T(8,128)(2,1)} copy(bf16[32,32,1024]{2,1,0:T(8,128)(2,1)} %bitcast.39) | data formatting | bytes 4194304
  19.7 12.4 %reshape.91 = bf16[1024,1024]{1,0:T(8,128)(2,1)} reshape(bf16[1024,32,32]{2,1,0:T(8,128)(2,1)} %bitcast.34) | data formatting | bytes 4194304
  32.1 0.0 reduce-scatter.4.cloned.1.call-update
  32.1 0.0 all-gather.6.cloned.1.call-start
  32.2 0.9 copy-done.5
  33.1 23.1 %all_to_all.57 = bf16[32,32,128]{2,1,0:T(8,128)(2,1)} all-to-all(bf16[32,32,128]{2,1,0:T(8,128)(2,1)S(1)} %copy-done.5), channel_id=1, replica_groups=mesh['shard'=32,'tensor'=4,'section'=2] {'shard'}, dimensions={0} | all-to-all | bytes 524288 | tf_op jit(solution)/shard_map/all_to_all | solution.py:82
  56.1 0.0 all-gather.6.cloned.1.call-update
  56.1 14.5 %reduce-scatter.4.cloned.1.call-done = bf16[128,1024]{1,0:T(8,128)(2,1)} async-done(((bf16[1024,1024]{1,0:T(8,128)(2,1)}), bf16[128,1024]{1,0:T(8,128)(2,1)}) %reduce-scatter.4.cloned.1.call-update) | async-done | bytes 262160
  70.6 1.8 reshape.92
  72.5 1.8 copy.32
  74.2 9.1 %all-to-all-start.1 = ((bf16[32,32,128]{2,1,0:T(8,128)(2,1)}), bf16[32,32,128]{2,1,0:T(8,128)(2,1)S(1)}, u32[]{:S(2)}, u32[]{:S(2)}) async-start(bf16[32,32,128]{2,1,0:T(8,128)(2,1)} %copy.32), calls=%async_computation.1 | async-start | bytes 524288 | tf_op jit(solution)/shard_map/all_to_all | solution.py:82
  83.3 0.0 all-gather.12.cloned.1.call-start
  83.4 19.8 %all-gather.6.cloned.1.call-done = bf16[1,1024,1024]{2,1,0:T(8,128)(2,1)} async-done(((bf16[1,1024,128]{2,1,0:T(8,128)(2,1)}), bf16[1,1024,1024]{2,1,0:T(8,128)(2,1)}) %all-gather.6.cloned.1.call-update) | async-done | bytes 2097168 | tf_op jit(solution)/shard_map/all_gather | solution.py:86
  103.2 3.0 fusion.2
  106.2 0.0 all-gather.12.cloned.1.call-update
  106.2 9.5 %all-to-all-start.2 = ((bf16[32,32,128]{2,1,0:T(8,128)(2,1)}), bf16[32,32,128]{2,1,0:T(8,128)(2,1)S(1)}, u32[]{:S(2)}, u32[]{:S(2)}) async-start(bf16[32,32,128]{2,1,0:T(8,128)(2,1)} %param.21), calls=%async_computation.2 | async-start | bytes 524288 | tf_op jit(solution)/shard_map/all_to_all | solution.py:82
  115.8 0.6 dynamic_slice.6
  116.4 2.3 multiply_reduce_fusion.1
  118.7 8.8 %all-to-all-done.2 = bf16[32,32,128]{2,1,0:T(8,128)(2,1)S(1)} async-done(((bf16[32,32,128]{2,1,0:T(8,128)(2,1)}), bf16[32,32,128]{2,1,0:T(8,128)(2,1)S(1)}, u32[]{:S(2)}, u32[]{:S(2)}) %all-to-all-start.2) | async-done | bytes 262176 | tf_op jit(solution)/shard_map/all_to_all | solution.py:82
  127.4 9.2 %all-gather.12.cloned.1.call-done = bf16[1024,1024]{1,0:T(8,128)(2,1)} async-done(((bf16[1024,128]{1,0:T(8,128)(2,1)}), bf16[1024,1024]{1,0:T(8,128)(2,1)}) %all-gather.12.cloned.1.call-update) | async-done | bytes 2097168 | tf_op jit(solution)/shard_map/all_gather | solution.py:91
  136.6 2.9 multiply_reduce_fusion
  139.5 0.4 copy.34
  140.0 0.5 broadcast.81
  140.5 2.2 reduce.2
  142.7 0.8 reshape.93
  143.5 9.5 %all-to-all-start.3 = ((bf16[32,2,2048]{2,1,0:T(2,128)(2,1)}), bf16[32,2,2048]{2,1,0:T(2,128)(2,1)S(1)}, u32[]{:S(2)}, u32[]{:S(2)}) async-start(bf16[32,2,2048]{2,1,0:T(2,128)(2,1)} %reshape.93), calls=%async_computation.3 | async-start | bytes 524288 | tf_op jit(solution)/shard_map/all_to_all | solution.py:96
  153.0 0.0 all-gather.8.cloned.1.call-start
  153.1 0.1 convert_reduce_fusion.1
  153.2 1.3 compare_select_fusion.2
  154.5 76.9 %all-reduce = (f32[5]{0:T(128)S(1)}, f32[5]{0:T(128)S(1)}) all-reduce(f32[5]{0:T(128)S(1)} %get-tuple-element.9, f32[5]{0:T(128)S(1)} %compare_select_fusion.2), channel_id=1, replica_groups=mesh['shard'=32,'tensor'=4,'section'=2] {'shard','tensor','section'}, use_global_device_ids=true, to_apply=%region_3.0 | all-reduce | flops 10 | bytes 80 | tf_op jit(solution)/shard_map/psum | solution.py:111
  231.4 0.1 select_reduce_fusion.1
  231.5 0.3 reshape.94
  231.8 0.5 bitcast_convert_fusion
  232.4 0.9 fusion.8
  233.3 0.0 all-gather.10.cloned.1.call-start
  233.3 0.2 convert_reduce_fusion
  233.5 0.1 select_reduce_fusion
  233.6 0.1 fusion.13
  233.7 1.7 gather_fusion
  235.4 0.3 select_select_fusion
  235.7 27.4 %all_to_all.58 = bf16[96,32,128]{2,1,0:T(8,128)(2,1)S(1)} all-to-all(bf16[96,32,128]{2,1,0:T(8,128)(2,1)S(1)} %select_select_fusion), channel_id=1, replica_groups=mesh['shard'=32,'tensor'=4,'section'=2] {'shard'}, dimensions={0} | all-to-all | bytes 1572864 | tf_op jit(solution)/shard_map/all_to_all | solution.py:82
  263.1 1.0 copy.28
  264.1 0.7 multiply_subtract_fusion
  264.8 44.7 %all-gather.10.cloned.1.call-done = bf16[3,1024,1024]{2,1,0:T(8,128)(2,1)} async-done(((bf16[3,1024,128]{2,1,0:T(8,128)(2,1)}), bf16[3,1024,1024]{2,1,0:T(8,128)(2,1)}) %all-gather.10.cloned.1.call-update) | async-done | bytes 6291472 | tf_op jit(solution)/shard_map/all_gather | solution.py:100
  309.5 6.5 %multiply_add_fusion = f32[3,1024,128]{2,1,0:T(8,128)} fusion(f32[3,1024,128]{2,1,0:T(8,128)S(1)} %copy-done.2, bf16[3,1024,1024]{2,1,0:T(8,128)(2,1)} %all-gather.10.cloned.1.call-done, bf16[3,1024,128]{2,1,0:T(8,128)(2,1)} %bitcast.36), kind=kOutput, calls=%fused_computation.3 | convolution fusion | flops 806486016 | bytes 10223616 | tf_op jit(solution)/shard_map/ski,skj->sij/dot_general | solution.py:106
  316.0 2.9 multiply_add_fusion.1
  319.0 1.3 copy.36
  (37 shorter events, 0.1 us)
Async XLA Ops:
  7.2 63.4 %reduce-scatter.4.cloned.1.call-start = ((), (), s32[]{:S(2)}) async-start(), calls=%async_computation.10 | async-start | bytes 2359296
  32.1 0.9 copy-start.5
  32.1 71.0 %all-gather.6.cloned.1.call-start = ((), (), s32[]{:S(2)}) async-start(), calls=%async_computation.6 | async-start | bytes 2359296 | tf_op jit(solution)/shard_map/all_gather | solution.py:86
  74.2 41.5 %copy-start.11 = (s32[32]{0:T(128)S(1)}, s32[32]{0:T(128)}, u32[]{:S(2)}) copy-start(s32[32]{0:T(128)} %param.23) | copy-start | bytes 388
  74.2 42.1 %copy-start.3 = (f32[32,32,128]{2,1,0:T(8,128)S(1)}, f32[32,32,128]{2,1,0:T(8,128)}, u32[]{:S(2)}) copy-start(f32[32,32,128]{2,1,0:T(8,128)} %param.16) | copy-start | bytes 1572868
  74.2 42.1 %copy-start.4 = (f32[32,32,128]{2,1,0:T(8,128)S(1)}, f32[32,32,128]{2,1,0:T(8,128)}, u32[]{:S(2)}) copy-start(f32[32,32,128]{2,1,0:T(8,128)} %param.17) | copy-start | bytes 1572868
  74.2 28.9 %all-to-all-start.1 = ((bf16[32,32,128]{2,1,0:T(8,128)(2,1)}), bf16[32,32,128]{2,1,0:T(8,128)(2,1)S(1)}, u32[]{:S(2)}, u32[]{:S(2)}) async-start(bf16[32,32,128]{2,1,0:T(8,128)(2,1)} %copy.32), calls=%async_computation.1 | async-start | bytes 524288 | tf_op jit(solution)/shard_map/all_to_all | solution.py:82
  83.3 53.3 %all-gather.12.cloned.1.call-start = ((), (), s32[]{:S(2)}) async-start(), calls=%async_computation.9 | async-start | bytes 2359296 | tf_op jit(solution)/shard_map/all_gather | solution.py:91
  106.2 21.2 %all-to-all-start.2 = ((bf16[32,32,128]{2,1,0:T(8,128)(2,1)}), bf16[32,32,128]{2,1,0:T(8,128)(2,1)S(1)}, u32[]{:S(2)}, u32[]{:S(2)}) async-start(bf16[32,32,128]{2,1,0:T(8,128)(2,1)} %param.21), calls=%async_computation.2 | async-start | bytes 524288 | tf_op jit(solution)/shard_map/all_to_all | solution.py:82
  139.5 92.8 %copy-start.6 = (bf16[32,32,128]{2,1,0:T(8,128)(2,1)S(1)}, bf16[32,32,128]{2,1,0:T(8,128)(2,1)}, u32[]{:S(2)}) copy-start(bf16[32,32,128]{2,1,0:T(8,128)(2,1)} %param.15) | copy-start | bytes 786436
  142.7 90.6 %copy-start.13 = (s32[32]{0:T(128)S(1)}, s32[32]{0:T(128)}, u32[]{:S(2)}) copy-start(s32[32]{0:T(128)} %param.22) | copy-start | bytes 388
  143.5 88.0 %all-to-all-start.3 = ((bf16[32,2,2048]{2,1,0:T(2,128)(2,1)}), bf16[32,2,2048]{2,1,0:T(2,128)(2,1)S(1)}, u32[]{:S(2)}, u32[]{:S(2)}) async-start(bf16[32,2,2048]{2,1,0:T(2,128)(2,1)} %reshape.93), calls=%async_computation.3 | async-start | bytes 524288 | tf_op jit(solution)/shard_map/all_to_all | solution.py:96
  153.0 111.8 %all-gather.8.cloned.1.call-start = ((), (), s32[]{:S(2)}) async-start(), calls=%async_computation.7 | async-start | bytes 2359296 | tf_op jit(solution)/shard_map/all_gather | solution.py:124
  233.3 76.2 %all-gather.10.cloned.1.call-start = ((), (), s32[]{:S(2)}) async-start(), calls=%async_computation.8 | async-start | bytes 7077888 | tf_op jit(solution)/shard_map/all_gather | solution.py:100
  235.7 28.4 %copy-start.7 = (f32[26,256]{1,0:T(8,128)S(1)}, f32[26,256]{1,0:T(8,128)}, u32[]{:S(2)}) copy-start(f32[26,256]{1,0:T(8,128)} %param.24) | copy-start | bytes 79876
  235.7 28.4 %copy-start.8 = (f32[26,256]{1,0:T(8,128)S(1)}, f32[26,256]{1,0:T(8,128)}, u32[]{:S(2)}) copy-start(f32[26,256]{1,0:T(8,128)} %param.26) | copy-start | bytes 79876
  235.7 28.4 %copy-start.9 = (f32[26,256]{1,0:T(8,128)S(1)}, f32[26,256]{1,0:T(8,128)}, u32[]{:S(2)}) copy-start(f32[26,256]{1,0:T(8,128)} %param.27) | copy-start | bytes 79876
  235.7 28.4 %copy-start.10 = (bf16[26,256]{1,0:T(8,128)(2,1)S(1)}, bf16[26,256]{1,0:T(8,128)(2,1)}, u32[]{:S(2)}) copy-start(bf16[26,256]{1,0:T(8,128)(2,1)} %param.25) | copy-start | bytes 39940
  235.7 73.7 %copy-start.2 = (f32[3,1024,128]{2,1,0:T(8,128)S(1)}, f32[3,1024,128]{2,1,0:T(8,128)}, u32[]{:S(2)}) copy-start(f32[3,1024,128]{2,1,0:T(8,128)} %param.19) | copy-start | bytes 4718596
  264.8 51.2 %copy-start.12 = (f32[3,1024,128]{2,1,0:T(8,128)S(1)}, f32[3,1024,128]{2,1,0:T(8,128)}, u32[]{:S(2)}) copy-start(f32[3,1024,128]{2,1,0:T(8,128)} %param.18) | copy-start | bytes 4718596
  309.5 6.5 %copy-start = (bf16[3,1024,1024]{2,1,0:T(8,128)(2,1)S(1)}, bf16[3,1024,1024]{2,1,0:T(8,128)(2,1)}, u32[]{:S(2)}) copy-start(bf16[3,1024,1024]{2,1,0:T(8,128)(2,1)} %all-gather.10.cloned.1.call-done) | copy-start | bytes 18874372
  316.0 3.0 copy-start.1
Sparse Core Ops, SparseCore 0:
  32.3 38.3 reduce-scatter.3
  72.4 30.6 all-gather.5
  106.3 30.2 all-gather.11
  233.4 25.8 all-gather.7
  264.2 45.2 all-gather.9
where the time goes:
time: 328 us; the launch traced here: 327 us
  blocking collectives  127 us (39%)
  waiting for transfers between devices  97 us (30%)
  local copies, waits for them, and re-layouts  35.9 us (11%)
  starting transfers between devices  28.4 us (9%)
  matrix products  15.4 us (5%)
  between operations  14 us (4%)
  other arithmetic  8.81 us (3%)
    psum x1, blocking collectives, shards(): lax.psum((adam_part, shampoo_part), ('shard', 'tensor', 'section'))  76.9 us
    all_to_all x2, blocking collectives, to_block(): return lax.all_to_all(x, 'shard', split_axis=0, concat_axis=1, tiled=True)  50.4 us
    all_gather x1, waiting for transfers between devices, shards(): lax.all_gather(slot_cols, ('tensor', 'section'), axis=2, tiled=True)  44.7 us
    unnamed x36, local copies, waits for them, and re-layouts  32.3 us
    all_gather x1, waiting for transfers between devices, shards(): lax.all_gather(left_cols, ('tensor', 'section'), axis=2, tiled=True)  19.8 us
    all_to_all x2, starting transfers between devices, to_block(): return lax.all_to_all(x, 'shard', split_axis=0, concat_axis=1, tiled=True)  18.6 us
    unnamed x6, waiting for transfers between devices  14.6 us
    all_to_all x1, starting transfers between devices, shards(): lax.all_to_all(precond.astype(jnp.bfloat16), 'shard', split_axis=1, conca...  9.54 us
  transfers between devices with their start and end apart: 8, of which 5 were waited for; matrix products, arithmetic and copies ran while one was open for 4% of the time, Pallas kernels for 0%

commit v1 on v0

--- a/solution.py
+++ b/solution.py
@@ -1,3 +1,4 @@
+import functools
 import jax
 import jax.numpy as jnp
 from jax import lax
@@ -14,6 +15,22 @@
 FLOOR_RATE = 1e-06
 CORRECT_ONE = 1.0 - 0.9**10
 CORRECT_TWO = 1.0 - 0.95**10
+
+
+def fix_records(work_x, d_out):
+    piece_out = jnp.concatenate(
+        lax.all_to_all(
+            jnp.stack([work_x] * lax.axis_size(("tensor", "section")), axis=0),
+            ("tensor", "section"),
+            0,
+            0,
+        ),
+        axis=d_out,
+    )
+    return piece_out
+
+
+_state_surface = functools.partial(fix_records, d_out=2)
 
 
 def adam_direction(grad_float, moment, second):
@@ -97,7 +114,7 @@
         precond.astype(jnp.bfloat16), "shard", split_axis=1, concat_axis=0, tiled=True
     ).astype(jnp.float32)
     slot_cols = to_block(fill_slots(gradient, block_ids, occupied))
-    grad_full = lax.all_gather(slot_cols, ("tensor", "section"), axis=2, tiled=True)
+    grad_full = _state_surface(slot_cols)
     first_row = group_index * slab_width
     grad_rows_own = lax.dynamic_slice_in_dim(grad_full, first_row, slab_width, 1)
     gram_left = jnp.einsum(

time: 328 us -> 355 us (1.082)
  blocking collectives: 127 us -> 155 us
  waiting for transfers between devices: 97 us -> 77.4 us
  starting transfers between devices: 28.4 us -> 38.2 us
  local copies, waits for them, and re-layouts: 35.9 us -> 44.7 us
    psum x1, blocking collectives: 76.9 us -> 131 us  [shards(): lax.psum((adam_part, shampoo_part), ('shard', 'tensor', 'section'))]
    all_gather x1 -> x0, waiting for transfers between devices: 44.7 us -> none  [shards(): lax.all_gather(slot_cols, ('tensor', 'section'), axis=2, tiled=True)]
    all_to_all x2 -> x1, blocking collectives: 50.4 us -> 23.1 us  [to_block(): return lax.all_to_all(x, 'shard', split_axis=0, concat_axis=1, tiled=True)]
    all_gather x1, waiting for transfers between devices: 0.01 us -> 10.6 us  [shards(): lax.all_gather(updated, ('tensor', 'section'), axis=2, tiled=True)]
    all_to_all x1, waiting for transfers between devices: 0.01 us -> 10.2 us  [shards(): lax.all_to_all(precond.astype(jnp.bfloat16), 'shard', split_axis=1, conca...]
    all_to_all x2 -> x3, waiting for transfers between devices: 8.75 us -> 17.6 us  [to_block(): return lax.all_to_all(x, 'shard', split_axis=0, concat_axis=1, tiled=True)]
    all_to_all x0 -> x1, starting transfers between devices: none -> 8.52 us  [fix_records(): lax.all_to_all(jnp.stack([work_x] * lax.axis_size(('tensor', 'section')),...]
    all_gather x1, waiting for transfers between devices: 9.22 us -> 4.71 us  [shards(): lax.all_gather(mixed, ('tensor', 'section'), axis=2, tiled=True)]
  transfers between devices with their start and end apart: 8 -> 9, of which waited for: 5 -> 7; matrix products, arithmetic and copies ran while one was open for 4% -> 10% of each run, Pallas kernels for 0% -> 0%
where the time goes in v1:
time: 355 us; the launch traced here: 354 us
  blocking collectives  155 us (44%)
  waiting for transfers between devices  77.4 us (22%)
  local copies, waits for them, and re-layouts  44.7 us (13%)
  starting transfers between devices  38.2 us (11%)
  matrix products  15.1 us (4%)
  between operations  14 us (4%)
  other arithmetic  9.74 us (3%)
    psum x1, blocking collectives, shards(): lax.psum((adam_part, shampoo_part), ('shard', 'tensor', 'section'))  131 us
    unnamed x32, local copies, waits for them, and re-layouts  34.2 us
    all_to_all x3, starting transfers between devices, to_block(): return lax.all_to_all(x, 'shard', split_axis=0, concat_axis=1, tiled=True)  23.2 us
    all_to_all x1, blocking collectives, to_block(): return lax.all_to_all(x, 'shard', split_axis=0, concat_axis=1, tiled=True)  23.1 us
    all_gather x1, waiting for transfers between devices, shards(): lax.all_gather(left_cols, ('tensor', 'section'), axis=2, tiled=True)  19.8 us
    all_to_all x3, waiting for transfers between devices, to_block(): return lax.all_to_all(x, 'shard', split_axis=0, concat_axis=1, tiled=True)  17.6 us
    unnamed x5, waiting for transfers between devices  14.5 us
    all_gather x1, waiting for transfers between devices, shards(): lax.all_gather(updated, ('tensor', 'section'), axis=2, tiled=True)  10.6 us
  transfers between devices with their start and end apart: 9, of which 7 were waited for; matrix products, arithmetic and copies ran while one was open for 10% of the time, Pallas kernels for 0%

profile of v1, /device:TPU:1, one launch (start us, length us, event | category | flops | bytes accessed | tf_op | source)
XLA Modules:
  0.0 353.7 jit_solution(9272582506453636841)
XLA Ops:
  7.2 0.0 reduce-scatter.4.cloned.1.call-start
  7.2 12.5 %copy.33 = bf16[32,32,1024]{1,0,2:T(8,128)(2,1)} copy(bf16[32,32,1024]{2,1,0:T(8,128)(2,1)} %bitcast.48) | data formatting | bytes 4194304
  19.7 12.4 %reshape.102 = bf16[1024,1024]{1,0:T(8,128)(2,1)} reshape(bf16[1024,32,32]{2,1,0:T(8,128)(2,1)} %bitcast.43) | data formatting | bytes 4194304
  32.1 0.0 all-gather.5.cloned.1.call-start
  32.2 0.9 copy-done.2
  33.1 23.1 %all_to_all.59 = bf16[32,32,128]{2,1,0:T(8,128)(2,1)} all-to-all(bf16[32,32,128]{2,1,0:T(8,128)(2,1)S(1)} %copy-done.2), channel_id=1, replica_groups=mesh['shard'=32,'tensor'=4,'section'=2] {'shard'}, dimensions={0} | all-to-all | bytes 524288 | tf_op jit(solution)/shard_map/all_to_all | solution.py:99
  56.2 14.5 %reduce-scatter.4.cloned.1.call-done = bf16[128,1024]{1,0:T(8,128)(2,1)} async-done(((bf16[1024,1024]{1,0:T(8,128)(2,1)}), bf16[128,1024]{1,0:T(8,128)(2,1)}) %reduce-scatter.4.cloned.1.call-update) | async-done | bytes 262160
  70.6 1.8 reshape.103
  72.5 1.8 copy.34
  74.2 9.1 %all-to-all-start.1 = ((bf16[32,32,128]{2,1,0:T(8,128)(2,1)}), bf16[32,32,128]{2,1,0:T(8,128)(2,1)S(1)}, u32[]{:S(2)}, u32[]{:S(2)}) async-start(bf16[32,32,128]{2,1,0:T(8,128)(2,1)} %copy.34), calls=%async_computation.1 | async-start | bytes 524288 | tf_op jit(solution)/shard_map/all_to_all | solution.py:99
  83.3 0.0 all-gather.9.cloned.1.call-start
  83.4 19.8 %all-gather.5.cloned.1.call-done = bf16[1,1024,1024]{2,1,0:T(8,128)(2,1)} async-done(((bf16[1,1024,128]{2,1,0:T(8,128)(2,1)}), bf16[1,1024,1024]{2,1,0:T(8,128)(2,1)}) %all-gather.5.cloned.1.call-update) | async-done | bytes 2097168 | tf_op jit(solution)/shard_map/all_gather | solution.py:103
  103.2 3.0 fusion.2
  106.2 9.6 %all-to-all-start.2 = ((bf16[32,32,128]{2,1,0:T(8,128)(2,1)}), bf16[32,32,128]{2,1,0:T(8,128)(2,1)S(1)}, u32[]{:S(2)}, u32[]{:S(2)}) async-start(bf16[32,32,128]{2,1,0:T(8,128)(2,1)} %param.21), calls=%async_computation.2 | async-start | bytes 524288 | tf_op jit(solution)/shard_map/all_to_all | solution.py:99
  115.8 0.2 convert_reduce_fusion
  116.0 0.1 select_reduce_fusion
  116.0 0.1 fusion.13
  116.2 1.7 gather_fusion
  117.8 1.2 select_select_fusion
  119.0 8.4 %all-to-all-done.2 = bf16[32,32,128]{2,1,0:T(8,128)(2,1)S(1)} async-done(((bf16[32,32,128]{2,1,0:T(8,128)(2,1)}), bf16[32,32,128]{2,1,0:T(8,128)(2,1)S(1)}, u32[]{:S(2)}, u32[]{:S(2)}) %all-to-all-start.2) | async-done | bytes 262176 | tf_op jit(solution)/shard_map/all_to_all | solution.py:99
  127.4 4.5 %all-to-all-start.4 = ((bf16[96,32,128]{2,1,0:T(8,128)(2,1)}), bf16[96,32,128]{2,1,0:T(8,128)(2,1)S(1)}, u32[]{:S(2)}, u32[]{:S(2)}) async-start(bf16[96,32,128]{2,1,0:T(8,128)(2,1)} %select_select_fusion), calls=%async_computation.4 | async-start | bytes 1572864 | tf_op jit(solution)/shard_map/all_to_all | solution.py:99
  132.0 4.7 %all-gather.9.cloned.1.call-done = bf16[1024,1024]{1,0:T(8,128)(2,1)} async-done(((bf16[1024,128]{1,0:T(8,128)(2,1)}), bf16[1024,1024]{1,0:T(8,128)(2,1)}) %all-gather.9.cloned.1.call-update) | async-done | bytes 2097168 | tf_op jit(solution)/shard_map/all_gather | solution.py:108
  136.7 2.9 multiply_reduce_fusion
  139.6 0.4 copy.39
  140.0 0.5 broadcast.82
  140.5 2.2 reduce.2
  142.7 0.8 reshape.104
  143.5 9.2 %all-to-all-done.4 = bf16[96,32,128]{2,1,0:T(8,128)(2,1)S(1)} async-done(((bf16[96,32,128]{2,1,0:T(8,128)(2,1)}), bf16[96,32,128]{2,1,0:T(8,128)(2,1)S(1)}, u32[]{:S(2)}, u32[]{:S(2)}) %all-to-all-start.4) | async-done | bytes 786464 | tf_op jit(solution)/shard_map/all_to_all | solution.py:99
  152.7 6.4 %all-to-all-start.3 = ((bf16[32,2,2048]{2,1,0:T(2,128)(2,1)}), bf16[32,2,2048]{2,1,0:T(2,128)(2,1)S(1)}, u32[]{:S(2)}, u32[]{:S(2)}) async-start(bf16[32,2,2048]{2,1,0:T(2,128)(2,1)} %reshape.104), calls=%async_computation.3 | async-start | bytes 524288 | tf_op jit(solution)/shard_map/all_to_all | solution.py:113
  159.0 0.1 copy.29
  159.1 10.2 %all-to-all-done.3 = bf16[32,2,2048]{2,1,0:T(2,128)(2,1)S(1)} async-done(((bf16[32,2,2048]{2,1,0:T(2,128)(2,1)}), bf16[32,2,2048]{2,1,0:T(2,128)(2,1)S(1)}, u32[]{:S(2)}, u32[]{:S(2)}) %all-to-all-start.3) | async-done | bytes 262176 | tf_op jit(solution)/shard_map/all_to_all | solution.py:113
  169.3 4.0 %stack.5 = bf16[8,3,1024,128]{3,2,1,0:T(8,128)(2,1)} broadcast(bf16[3,1024,128]{2,1,0:T(8,128)(2,1)S(1)} %bitcast.45), dimensions={1,2,3} | broadcast | bytes 7077888 | tf_op jit(solution)/shard_map/stack | solution.py:23
  173.3 8.5 %all-to-all-start.5 = ((bf16[8,3,1024,128]{3,2,1,0:T(8,128)(2,1)}), bf16[8,3,1024,128]{3,2,1,0:T(8,128)(2,1)}, u32[]{:S(2)}, u32[]{:S(2)}) async-start(bf16[8,3,1024,128]{3,2,1,0:T(8,128)(2,1)} %stack.5), calls=%async_computation.5 | async-start | bytes 12582912 | tf_op jit(solution)/shard_map/all_to_all | solution.py:22
  181.8 0.6 dynamic_slice.6
  182.4 2.4 multiply_reduce_fusion.1
  184.8 0.1 convert_reduce_fusion.1
  184.9 1.3 compare_select_fusion.2
  186.2 131.5 %all-reduce = (f32[5]{0:T(128)S(1)}, f32[5]{0:T(128)S(1)}) all-reduce(f32[5]{0:T(128)S(1)} %get-tuple-element.9, f32[5]{0:T(128)S(1)} %compare_select_fusion.2), channel_id=1, replica_groups=mesh['shard'=32,'tensor'=4,'section'=2] {'shard','tensor','section'}, use_global_device_ids=true, to_apply=%region_3.0 | all-reduce | flops 10 | bytes 80 | tf_op jit(solution)/shard_map/psum | solution.py:128
  317.7 0.1 select_reduce_fusion.1
  317.8 0.3 reshape.105
  318.1 0.5 bitcast_convert_fusion
  318.7 0.9 fusion.8
  319.6 0.7 multiply_subtract_fusion
  320.3 3.9 %copy_bitcast_fusion = bf16[3,1024,1024]{2,1,0:T(8,128)(2,1)S(1)} fusion(bf16[8,3,1024,128]{3,2,1,0:T(8,128)(2,1)} %all-to-all-done.5), kind=kLoop, calls=%fused_computation.1 | loop fusion | bytes 12582912 | tf_op jit(solution)/shard_map/reshape | solution.py:21
  324.2 3.0 multiply_add_fusion.1
  327.1 6.3 %multiply_add_fusion = f32[3,1024,128]{2,1,0:T(8,128)} fusion(f32[3,1024,128]{2,1,0:T(8,128)S(1)} %copy-done.10, bf16[3,1024,128]{2,1,0:T(8,128)(2,1)S(1)} %bitcast.46, bf16[8,3,1024,128]{3,2,1,0:T(8,128)(2,1)} %all-to-all-done.5), kind=kOutput, calls=%fused_computation.4 | convolution fusion | flops 806486016 | bytes 10223616 | tf_op jit(solution)/shard_map/ski,skj->sij/dot_general | solution.py:123
  333.4 10.6 %all-gather.7.cloned.1.call-done = bf16[32,32,1024]{2,1,0:T(8,128)(2,1)} async-done(((bf16[32,32,128]{2,1,0:T(8,128)(2,1)}), bf16[32,32,1024]{2,1,0:T(8,128)(2,1)}) %all-gather.7.cloned.1.call-update) | async-done | bytes 2097168 | tf_op jit(solution)/shard_map/all_gather | solution.py:141
  344.0 3.2 copy.41
  (35 shorter events, 0.2 us)
Async XLA Ops:
  7.2 63.5 %reduce-scatter.4.cloned.1.call-start = ((), (), s32[]{:S(2)}) async-start(), calls=%async_computation.10 | async-start | bytes 2359296
  32.1 0.9 copy-start.2
  32.1 71.0 %all-gather.5.cloned.1.call-start = ((), (), s32[]{:S(2)}) async-start(), calls=%async_computation.7 | async-start | bytes 2359296 | tf_op jit(solution)/shard_map/all_gather | solution.py:103
  74.2 41.5 %copy-start.11 = (s32[32]{0:T(128)S(1)}, s32[32]{0:T(128)}, u32[]{:S(2)}) copy-start(s32[32]{0:T(128)} %param.22) | copy-start | bytes 388
  74.2 28.9 %all-to-all-start.1 = ((bf16[32,32,128]{2,1,0:T(8,128)(2,1)}), bf16[32,32,128]{2,1,0:T(8,128)(2,1)S(1)}, u32[]{:S(2)}, u32[]{:S(2)}) async-start(bf16[32,32,128]{2,1,0:T(8,128)(2,1)} %copy.34), calls=%async_computation.1 | async-start | bytes 524288 | tf_op jit(solution)/shard_map/all_to_all | solution.py:99
  83.3 53.3 %all-gather.9.cloned.1.call-start = ((), (), s32[]{:S(2)}) async-start(), calls=%async_computation.9 | async-start | bytes 2359296 | tf_op jit(solution)/shard_map/all_gather | solution.py:108
  106.2 21.2 %all-to-all-start.2 = ((bf16[32,32,128]{2,1,0:T(8,128)(2,1)}), bf16[32,32,128]{2,1,0:T(8,128)(2,1)S(1)}, u32[]{:S(2)}, u32[]{:S(2)}) async-start(bf16[32,32,128]{2,1,0:T(8,128)(2,1)} %param.21), calls=%async_computation.2 | async-start | bytes 524288 | tf_op jit(solution)/shard_map/all_to_all | solution.py:99
  127.4 25.2 %all-to-all-start.4 = ((bf16[96,32,128]{2,1,0:T(8,128)(2,1)}), bf16[96,32,128]{2,1,0:T(8,128)(2,1)S(1)}, u32[]{:S(2)}, u32[]{:S(2)}) async-start(bf16[96,32,128]{2,1,0:T(8,128)(2,1)} %select_select_fusion), calls=%async_computation.4 | async-start | bytes 1572864 | tf_op jit(solution)/shard_map/all_to_all | solution.py:99
  152.7 16.6 %all-to-all-start.3 = ((bf16[32,2,2048]{2,1,0:T(2,128)(2,1)}), bf16[32,2,2048]{2,1,0:T(2,128)(2,1)S(1)}, u32[]{:S(2)}, u32[]{:S(2)}) async-start(bf16[32,2,2048]{2,1,0:T(2,128)(2,1)} %reshape.104), calls=%async_computation.3 | async-start | bytes 524288 | tf_op jit(solution)/shard_map/all_to_all | solution.py:113
  173.3 8.5 %copy-start.8 = (s32[32]{0:T(128)S(1)}, s32[32]{0:T(128)}, u32[]{:S(2)}) copy-start(s32[32]{0:T(128)} %param.23) | copy-start | bytes 388
  173.3 9.1 %copy-start = (f32[32,32,128]{2,1,0:T(8,128)S(1)}, f32[32,32,128]{2,1,0:T(8,128)}, u32[]{:S(2)}) copy-start(f32[32,32,128]{2,1,0:T(8,128)} %param.16) | copy-start | bytes 1572868
  173.3 9.1 %copy-start.1 = (f32[32,32,128]{2,1,0:T(8,128)S(1)}, f32[32,32,128]{2,1,0:T(8,128)}, u32[]{:S(2)}) copy-start(f32[32,32,128]{2,1,0:T(8,128)} %param.17) | copy-start | bytes 1572868
  173.3 147.0 %all-to-all-start.5 = ((bf16[8,3,1024,128]{3,2,1,0:T(8,128)(2,1)}), bf16[8,3,1024,128]{3,2,1,0:T(8,128)(2,1)}, u32[]{:S(2)}, u32[]{:S(2)}) async-start(bf16[8,3,1024,128]{3,2,1,0:T(8,128)(2,1)} %stack.5), calls=%async_computation.5 | async-start | bytes 12582912 | tf_op jit(solution)/shard_map/all_to_all | solution.py:22
  181.8 162.2 %all-gather.7.cloned.1.call-start = ((), (), s32[]{:S(2)}) async-start(), calls=%async_computation.8 | async-start | bytes 2359296 | tf_op jit(solution)/shard_map/all_gather | solution.py:141
  182.4 136.3 %copy-start.3 = (bf16[32,32,128]{2,1,0:T(8,128)(2,1)S(1)}, bf16[32,32,128]{2,1,0:T(8,128)(2,1)}, u32[]{:S(2)}) copy-start(bf16[32,32,128]{2,1,0:T(8,128)(2,1)} %param.15) | copy-start | bytes 786436
  184.8 134.8 %copy-start.4 = (f32[26,256]{1,0:T(8,128)S(1)}, f32[26,256]{1,0:T(8,128)}, u32[]{:S(2)}) copy-start(f32[26,256]{1,0:T(8,128)} %param.24) | copy-start | bytes 79876
  184.8 134.8 %copy-start.5 = (f32[26,256]{1,0:T(8,128)S(1)}, f32[26,256]{1,0:T(8,128)}, u32[]{:S(2)}) copy-start(f32[26,256]{1,0:T(8,128)} %param.26) | copy-start | bytes 79876
  184.8 134.8 %copy-start.6 = (f32[26,256]{1,0:T(8,128)S(1)}, f32[26,256]{1,0:T(8,128)}, u32[]{:S(2)}) copy-start(f32[26,256]{1,0:T(8,128)} %param.27) | copy-start | bytes 79876
  184.8 134.8 %copy-start.7 = (bf16[26,256]{1,0:T(8,128)(2,1)S(1)}, bf16[26,256]{1,0:T(8,128)(2,1)}, u32[]{:S(2)}) copy-start(bf16[26,256]{1,0:T(8,128)(2,1)} %param.25) | copy-start | bytes 39940
  320.3 3.9 %copy-start.9 = (f32[3,1024,128]{2,1,0:T(8,128)S(1)}, f32[3,1024,128]{2,1,0:T(8,128)}, u32[]{:S(2)}) copy-start(f32[3,1024,128]{2,1,0:T(8,128)} %param.18) | copy-start | bytes 4718596
  324.1 3.0 copy-start.10
Sparse Core Ops, SparseCore 0:
  32.3 38.3 reduce-scatter.3
  72.5 30.6 all-gather.4
  106.3 30.2 all-gather.8
  319.7 24.2 all-gather.6
